TPU v7x, 32 devices: a whole 2x2x4 slice. The times are simulated.
32 devices in a mesh: row: 4 (over y, x), col: 8 (over z, core).
Axes of the slice: x: 2, y: 2, z: 4, core: 2. Of those that a mesh axis runs over, the one named last changes fastest.
Arguments:
- out_grad: bfloat16 [4096, 8192], P('row', 'col'), may hold values from -0.059814453 to 0.059814453
- hidden: bfloat16 [4096, 28672], P('row', 'col'), may hold values from -6 to 6
- basis: bfloat16 [8192, 1024], P('col'), may hold values from -0.0625 to 0.0625
- weight: bfloat16 [8192, 28672], P('row', 'col'), may hold values from -6 to 6
- first_moment: float32 [1024, 28672], P('row', 'col'), may hold values from -4 to 4
- second_moment: float32 [1024, 28672], P('row', 'col'), may hold values from 0.25 to 4
Outputs:
- new_weight: bfloat16 [8192, 28672], P('row', 'col')
- new_first: float32 [1024, 28672], P('row', 'col')
- new_second: float32 [1024, 28672], P('row', 'col')
All inputs are finite; a program needn't handle non-finite values.
Results may differ from a plain program's by a relative error of at most 0.0039.
Values may be sent and summed in bfloat16 or wider, within the bound.
A program may use at most 128 MiB of HBM per device.

v0:
```python
import jax
import jax.numpy as jnp
from jax import lax
from jax.sharding import PartitionSpec as P

STEP_COUNT = 1000
beta_one = 0.9
beta_two = 0.999
epsilon = 1e-08
step_size = 1.0


def spread(block, axis, source):
    block = jnp.where(lax.axis_index(axis) == source, block, jnp.zeros_like(block))
    return lax.psum(block, axis)


def local(out_grad, hidden, basis, weight, first_moment, second_moment):
    partial_value = jnp.dot(out_grad, basis, preferred_element_type=jnp.float32)
    projected = lax.psum(partial_value, "col").astype(jnp.bfloat16)
    columns = projected
    gradient = lax.psum_scatter(
        lax.dot_general(
            columns, hidden, (((0,), (0,)), ((), ())), preferred_element_type=jnp.float32
        ).astype(jnp.bfloat16),
        "row",
        scatter_dimension=0,
        tiled=True,
    ).astype(jnp.float32)
    new_first = beta_one * first_moment + (1.0 - beta_one) * gradient
    new_second = beta_two * second_moment + (1.0 - beta_two) * gradient * gradient
    first_hat = new_first / (1.0 - beta_one**STEP_COUNT)
    second_hat = new_second / (1.0 - beta_two**STEP_COUNT)
    direction = (first_hat / (jnp.sqrt(second_hat) + epsilon)).astype(jnp.bfloat16)
    per_band = lax.axis_size("col") // lax.axis_size("row")
    blocks = [
        spread(basis, "col", lax.axis_index("row") * per_band + offset)
        for offset in range(per_band)
    ]
    local_basis = jnp.concatenate(blocks, 0)
    initial = jnp.zeros((local_basis.shape[0], direction.shape[1]), jnp.float32)
    portion = lax.all_gather(direction, "row", axis=0, tiled=True)
    columns = lax.slice_in_dim(local_basis, 0, portion.shape[0], axis=1)
    update = initial + jnp.dot(columns, portion, preferred_element_type=jnp.float32)
    new_weight = (weight.astype(jnp.float32) - step_size * update).astype(jnp.bfloat16)
    return (new_weight, new_first, new_second)


def solution(mesh):
    in_specs = (
        P("row", "col"),
        P("row", "col"),
        P("col", None),
        P("row", "col"),
        P("row", "col"),
        P("row", "col"),
    )
    out_specs = (P("row", "col"), P("row", "col"), P("row", "col"))
    return jax.shard_map(local, mesh=mesh, in_specs=in_specs, out_specs=out_specs, check_vma=False)
```

profile of v0, /device:TPU:0, one launch (start us, length us, event | category | flops | bytes accessed | tf_op | source)
XLA Modules:
  0.0 316.9 jit_solution(15711441214757857168)
XLA Ops:
  8.0 0.0 copy-start
  8.0 0.0 reduce-scatter.2.cloned.1.call-start
  8.1 1.5 copy-done
  9.6 5.9 %fusion.9 = f32[1024,1024]{1,0:T(8,128)} fusion(bf16[1024,1024]{1,0:T(8,128)(2,1)S(1)} %copy-done, bf16[1024,1024]{1,0:T(8,128)(2,1)} %param.8), kind=kOutput, calls=%fused_computation.14 | convolution fusion | flops 2147483648 | bytes 8388608 | tf_op jit(solution)/shard_map/dot_general | solution.py:19
  15.5 90.6 %all-reduce.5 = bf16[1024,1024]{1,0:T(8,128)(2,1)S(1)} all-reduce(f32[1024,1024]{1,0:T(8,128)} %fusion.9), channel_id=1, replica_groups=mesh['row'=4,'col'=8] {'col'}, use_global_device_ids=true, to_apply=%region_2.3 | all-reduce | flops 1048576 | bytes 6291456 | tf_op jit(solution)/shard_map/psum | solution.py:20
  106.1 13.0 %convolution_convert_fusion = bf16[1024,3584]{1,0:T(8,128)(2,1)} fusion(bf16[1024,3584]{1,0:T(8,128)(2,1)} %param.7, bf16[1024,1024]{1,0:T(8,128)(2,1)S(1)} %all-reduce.5), kind=kOutput, calls=%fused_computation.1 | convolution fusion | flops 7519862784 | bytes 16777216 | tf_op jit(solution)/shard_map/dot_general | solution.py:23
  119.1 0.0 copy-start.2
  119.1 0.0 reduce-scatter.2.cloned.1.call-update
  119.1 0.0 all-reduce.4.cloned.1.call-start
  119.2 1.5 copy-done.2
  120.7 2.3 broadcast_select_fusion.1
  123.0 0.0 all-reduce.4.cloned.1.call-update
  123.0 0.2 all-gather.2.cloned.1.call-start
  123.3 74.2 %reduce-scatter.2.cloned.1.call-done = bf16[256,3584]{1,0:T(8,128)(2,1)} async-done(((bf16[1024,3584]{1,0:T(8,128)(2,1)}), bf16[256,3584]{1,0:T(8,128)(2,1)}) %reduce-scatter.2.cloned.1.call-update) | async-done | bytes 1835024 | tf_op jit(solution)/shard_map/reduce_scatter | solution.py:22
  197.5 8.8 %divide_convert_fusion = (bf16[256,3584]{1,0:T(8,128)(2,1)}, f32[256,3584]{1,0:T(8,128)}, f32[256,3584]{1,0:T(8,128)}) fusion(bf16[256,3584]{1,0:T(8,128)(2,1)} %reduce-scatter.2.cloned.1.call-done, f32[256,3584]{1,0:T(8,128)} %param.11, f32[256,3584]{1,0:T(8,128)} %param.10), kind=kLoop, calls=%fused_computation.9 | loop fusion | flops 11010048 | bytes 18350080 | tf_op jit(solution)/shard_map/convert_element_type | solution.py:34
  206.4 0.0 all-gather.2.cloned.1.call-update
  206.4 12.6 %all-reduce.4.cloned.1.call-done = (bf16[1024,1024]{1,0:T(8,128)(2,1)}, bf16[1024,1024]{1,0:T(8,128)(2,1)}) async-done(((bf16[1024,1024]{1,0:T(8,128)(2,1)}, bf16[1024,1024]{1,0:T(8,128)(2,1)}), (bf16[1024,1024]{1,0:T(8,128)(2,1)}, bf16[1024,1024]{1,0:T(8,128)(2,1)})) %all-reduce.4.cloned.1.call-update) | async-done | bytes 4194320 | tf_op jit(solution)/shard_map/psum | solution.py:15
  219.0 66.3 %all-gather.2.cloned.1.call-done = bf16[1024,3584]{1,0:T(8,128)(2,1)} async-done(((bf16[256,3584]{1,0:T(8,128)(2,1)}), bf16[1024,3584]{1,0:T(8,128)(2,1)}) %all-gather.2.cloned.1.call-update) | async-done | bytes 7340048 | tf_op jit(solution)/shard_map/all_gather | solution.py:42
  285.3 0.0 copy-start.1
  285.3 24.2 %subtract_convert_fusion = bf16[2048,3584]{1,0:T(8,128)(2,1)} fusion(bf16[2048,3584]{1,0:T(8,128)(2,1)} %param.9, bf16[1024,3584]{1,0:T(8,128)(2,1)} %all-gather.2.cloned.1.call-done, bf16[1024,1024]{1,0:T(8,128)(2,1)} %get-tuple-element.3, bf16[1024,1024]{1,0:T(8,128)(2,1)} %get-tuple-element.4), kind=kOutput, calls=%fused_computation | convolution fusion | flops 15062794240 | bytes 40894464 | tf_op jit(solution)/shard_map/dot_general | solution.py:44
  309.5 0.0 copy-done.1
Async XLA Ops:
  8.0 1.6 copy-start
  8.0 189.5 %reduce-scatter.2.cloned.1.call-start = ((), (), s32[]{:S(2)}) async-start(), calls=%async_computation.1 | async-start | bytes 9175040 | tf_op jit(solution)/shard_map/reduce_scatter | solution.py:22
  119.1 1.6 copy-start.2
  119.1 99.9 %all-reduce.4.cloned.1.call-start = ((), (), s32[]{:S(2)}) async-start(), calls=%async_computation.3 | async-start | bytes 8388608 | tf_op jit(solution)/shard_map/psum | solution.py:15
  123.0 162.2 %all-gather.2.cloned.1.call-start = ((), (), s32[]{:S(2)}) async-start(), calls=%async_computation.2 | async-start | bytes 9175040 | tf_op jit(solution)/shard_map/all_gather | solution.py:42
  285.3 24.2 %copy-start.1 = (bf16[1024,1024]{1,0:T(8,128)(2,1)S(1)}, bf16[1024,1024]{1,0:T(8,128)(2,1)}, u32[]{:S(2)}) copy-start(bf16[1024,1024]{1,0:T(8,128)(2,1)} %param.6) | copy-start | bytes 6291460
Sparse Core Ops, SparseCore 0:
  119.3 78.2 reduce-scatter.1
  206.5 78.7 all-gather.1
Sparse Core Ops, SparseCore 1:
  123.1 95.8 all-reduce.3
where the time goes:
time: 317 us
  waiting for transfers between devices  153 us (48%)
  blocking collectives  90.6 us (29%)
  matrix products  43.1 us (14%)
  between operations  15.5 us (5%)
  other arithmetic  11.1 us (4%)
    psum x1, blocking collectives, local(): projected = lax.psum(partial_value, 'col').astype(jnp.bfloat16)  90.6 us
    reduce_scatter x1, waiting for transfers between devices, local(): lax.psum_scatter(lax.dot_general(columns, hidden, (((0,), (0,)), ((), ())...  74.2 us
    all_gather x1, waiting for transfers between devices, local(): portion = lax.all_gather(direction, 'row', axis=0, tiled=True)  66.3 us
    dot_general x1, matrix products, local(): jnp.dot(columns, portion, preferred_element_type=jnp.float32)  24.2 us
    dot_general x1, matrix products, local(): lax.dot_general(columns, hidden, (((0,), (0,)), ((), ())), preferred_elem...  13 us
    psum x1, waiting for transfers between devices, spread(): return lax.psum(block, axis)  12.6 us
    convert_element_type x1, other arithmetic, local(): (first_hat / (jnp.sqrt(second_hat) + epsilon)).astype(jnp.bfloat16)  8.84 us
  transfers between devices with their start and end apart: 3, of which 3 were waited for; matrix products, arithmetic and copies ran while one was open for 4% of the time, Pallas kernels for 0%

commit v1 on v0

--- a/solution.py
+++ b/solution.py
@@ -17,7 +17,7 @@
 
 def local(out_grad, hidden, basis, weight, first_moment, second_moment):
     partial_value = jnp.dot(out_grad, basis, preferred_element_type=jnp.float32)
-    projected = lax.psum(partial_value, "col").astype(jnp.bfloat16)
+    projected = jnp.sum(lax.all_gather(partial_value, "col"), axis=0).astype(jnp.bfloat16)
     columns = projected
     gradient = lax.psum_scatter(
         lax.dot_general(

time: 317 us -> 620 us (1.96)
  waiting for transfers between devices: 153 us -> 536 us
  blocking collectives: 90.6 us -> 0 us
  other arithmetic: 11.1 us -> 23.9 us
    all_gather x0 -> x1, waiting for transfers between devices: none -> 291 us  [local(): lax.all_gather(partial_value, 'col')]
    psum x1 -> x0, blocking collectives: 90.6 us -> none  [local(): projected = lax.psum(partial_value, 'col').astype(jnp.bfloat16)]
    psum x1, waiting for transfers between devices: 12.6 us -> 90.2 us  [spread(): return lax.psum(block, axis)]
    all_gather x1, waiting for transfers between devices: 66.3 us -> 81.1 us  [local(): portion = lax.all_gather(direction, 'row', axis=0, tiled=True)]
    reduce_sum x0 -> x1, other arithmetic: none -> 12.9 us  [local(): jnp.sum(lax.all_gather(partial_value, 'col'), axis=0).astype(jnp.bfloat16)]
  transfers between devices with their start and end apart: 3 -> 4, of which waited for: 3 -> 4; matrix products, arithmetic and copies ran while one was open for 4% -> 2% of each run, Pallas kernels for 0% -> 0%
where the time goes in v1:
time: 620 us
  waiting for transfers between devices  536 us (86%)
  matrix products  43.1 us (7%)
  other arithmetic  23.9 us (4%)
  between operations  13.8 us (2%)
    all_gather x1, waiting for transfers between devices, local(): lax.all_gather(partial_value, 'col')  291 us
    psum x1, waiting for transfers between devices, spread(): return lax.psum(block, axis)  90.2 us
    all_gather x1, waiting for transfers between devices, local(): portion = lax.all_gather(direction, 'row', axis=0, tiled=True)  81.1 us
    reduce_scatter x1, waiting for transfers between devices, local(): lax.psum_scatter(lax.dot_general(columns, hidden, (((0,), (0,)), ((), ())...  73 us
    dot_general x1, matrix products, local(): jnp.dot(columns, portion, preferred_element_type=jnp.float32)  24.2 us
    dot_general x1, matrix products, local(): lax.dot_general(columns, hidden, (((0,), (0,)), ((), ())), preferred_elem...  13 us
    reduce_sum x1, other arithmetic, local(): jnp.sum(lax.all_gather(partial_value, 'col'), axis=0).astype(jnp.bfloat16)  12.9 us
  transfers between devices with their start and end apart: 4, of which 4 were waited for; matrix products, arithmetic and copies ran while one was open for 2% of the time, Pallas kernels for 0%

profile of v1, /device:TPU:0, one launch (start us, length us, event | category | flops | bytes accessed | tf_op | source)
XLA Modules:
  0.0 620.0 jit_solution(4130490073210630273)
XLA Ops:
  7.2 0.0 copy-start
  7.2 0.0 all-gather.6.cloned.1.call-start
  7.2 1.5 copy-done
  8.8 5.9 fusion.9
  14.7 0.0 all-gather.6.cloned.1.call-update
  14.7 0.0 reduce-scatter.2.cloned.1.call-start
  14.8 291.4 %all-gather.6.cloned.1.call-done = f32[8192,1024]{1,0:T(8,128)} async-done(((f32[1024,1024]{1,0:T(8,128)}), f32[8192,1024]{1,0:T(8,128)}) %all-gather.6.cloned.1.call-update) | async-done | bytes 33554448 | tf_op jit(solution)/shard_map/all_gather | solution.py:20
  306.2 12.9 %reduce_sum.9 = bf16[1024,1024]{1,0:T(8,128)(2,1)S(1)} reduce(f32[8,1024,1024]{2,1,0:T(8,128)} %bitcast.6, f32[]{:T(128)} %constant.8.clone.1), dimensions={0}, to_apply=%region_2.3 | reduce | flops 7340032 | bytes 35651588 | tf_op jit(solution)/shard_map/reduce_sum | solution.py:20
  319.1 13.0 %convolution_convert_fusion = bf16[1024,3584]{1,0:T(8,128)(2,1)} fusion(bf16[1024,3584]{1,0:T(8,128)(2,1)} %param.7, bf16[1024,1024]{1,0:T(8,128)(2,1)S(1)} %reduce_sum.9), kind=kOutput, calls=%fused_computation.1 | convolution fusion | flops 7519862784 | bytes 16777216 | tf_op jit(solution)/shard_map/dot_general | solution.py:23
  332.1 0.0 copy-start.2
  332.1 0.0 reduce-scatter.2.cloned.1.call-update
  332.1 0.0 all-reduce.3.cloned.1.call-start
  332.1 1.5 copy-done.2
  333.7 2.3 broadcast_select_fusion.1
  336.0 0.0 all-reduce.3.cloned.1.call-update
  336.0 0.2 all-gather.4.cloned.1.call-start
  336.2 73.0 %reduce-scatter.2.cloned.1.call-done = bf16[256,3584]{1,0:T(8,128)(2,1)} async-done(((bf16[1024,3584]{1,0:T(8,128)(2,1)}), bf16[256,3584]{1,0:T(8,128)(2,1)}) %reduce-scatter.2.cloned.1.call-update) | async-done | bytes 1835024 | tf_op jit(solution)/shard_map/reduce_scatter | solution.py:22
  409.2 8.8 %divide_convert_fusion = (bf16[256,3584]{1,0:T(8,128)(2,1)}, f32[256,3584]{1,0:T(8,128)}, f32[256,3584]{1,0:T(8,128)}) fusion(bf16[256,3584]{1,0:T(8,128)(2,1)} %reduce-scatter.2.cloned.1.call-done, f32[256,3584]{1,0:T(8,128)} %param.11, f32[256,3584]{1,0:T(8,128)} %param.10), kind=kLoop, calls=%fused_computation.9 | loop fusion | flops 11010048 | bytes 18350080 | tf_op jit(solution)/shard_map/convert_element_type | solution.py:34
  417.9 0.0 all-gather.4.cloned.1.call-update
  418.0 90.2 %all-reduce.3.cloned.1.call-done = (bf16[1024,1024]{1,0:T(8,128)(2,1)}, bf16[1024,1024]{1,0:T(8,128)(2,1)}) async-done(((bf16[1024,1024]{1,0:T(8,128)(2,1)}, bf16[1024,1024]{1,0:T(8,128)(2,1)}), (bf16[1024,1024]{1,0:T(8,128)(2,1)}, bf16[1024,1024]{1,0:T(8,128)(2,1)})) %all-reduce.3.cloned.1.call-update) | async-done | bytes 4194320 | tf_op jit(solution)/shard_map/psum | solution.py:15
  508.1 81.1 %all-gather.4.cloned.1.call-done = bf16[1024,3584]{1,0:T(8,128)(2,1)} async-done(((bf16[256,3584]{1,0:T(8,128)(2,1)}), bf16[1024,3584]{1,0:T(8,128)(2,1)}) %all-gather.4.cloned.1.call-update) | async-done | bytes 7340048 | tf_op jit(solution)/shard_map/all_gather | solution.py:42
  589.2 0.0 copy-start.1
  589.2 24.2 %subtract_convert_fusion = bf16[2048,3584]{1,0:T(8,128)(2,1)} fusion(bf16[2048,3584]{1,0:T(8,128)(2,1)} %param.9, bf16[1024,3584]{1,0:T(8,128)(2,1)} %all-gather.4.cloned.1.call-done, bf16[1024,1024]{1,0:T(8,128)(2,1)} %get-tuple-element.3, bf16[1024,1024]{1,0:T(8,128)(2,1)} %get-tuple-element.4), kind=kOutput, calls=%fused_computation | convolution fusion | flops 15062794240 | bytes 40894464 | tf_op jit(solution)/shard_map/dot_general | solution.py:44
  613.5 0.0 copy-done.1
Async XLA Ops:
  7.2 1.6 copy-start
  7.2 299.0 %all-gather.6.cloned.1.call-start = ((), (), s32[]{:S(2)}) async-start(), calls=%async_computation.3 | async-start | bytes 37748736 | tf_op jit(solution)/shard_map/all_gather | solution.py:20
  14.7 394.5 %reduce-scatter.2.cloned.1.call-start = ((), (), s32[]{:S(2)}) async-start(), calls=%async_computation.1 | async-start | bytes 9175040 | tf_op jit(solution)/shard_map/reduce_scatter | solution.py:22
  332.1 1.6 copy-start.2
  332.1 176.0 %all-reduce.3.cloned.1.call-start = ((), (), s32[]{:S(2)}) async-start(), calls=%async_computation.4 | async-start | bytes 8388608 | tf_op jit(solution)/shard_map/psum | solution.py:15
  336.0 253.2 %all-gather.4.cloned.1.call-start = ((), (), s32[]{:S(2)}) async-start(), calls=%async_computation.2 | async-start | bytes 9175040 | tf_op jit(solution)/shard_map/all_gather | solution.py:42
  589.2 24.2 %copy-start.1 = (bf16[1024,1024]{1,0:T(8,128)(2,1)S(1)}, bf16[1024,1024]{1,0:T(8,128)(2,1)}, u32[]{:S(2)}) copy-start(bf16[1024,1024]{1,0:T(8,128)(2,1)} %param.6) | copy-start | bytes 6291460
Sparse Core Ops, SparseCore 0:
  14.8 291.3 all-gather.5
  332.2 76.9 reduce-scatter.1
  411.6 96.4 all-reduce.2
  510.4 78.7 all-gather.3

commit v2 on v0

--- a/solution.py
+++ b/solution.py
@@ -39,7 +39,9 @@
     ]
     local_basis = jnp.concatenate(blocks, 0)
     initial = jnp.zeros((local_basis.shape[0], direction.shape[1]), jnp.float32)
-    portion = lax.all_gather(direction, "row", axis=0, tiled=True)
+    portion = jnp.concatenate(
+        lax.all_to_all(jnp.stack([direction] * lax.axis_size("row")), "row", 0, 0), axis=0
+    )
     columns = lax.slice_in_dim(local_basis, 0, portion.shape[0], axis=1)
     update = initial + jnp.dot(columns, portion, preferred_element_type=jnp.float32)
     new_weight = (weight.astype(jnp.float32) - step_size * update).astype(jnp.bfloat16)

time: 317 us -> 348 us (1.098)
  waiting for transfers between devices: 153 us -> 176 us
  starting transfers between devices: 0.3 us -> 5.83 us
    psum x1, waiting for transfers between devices: 12.6 us -> 98.1 us  [spread(): return lax.psum(block, axis)]
    all_gather x1 -> x0, waiting for transfers between devices: 66.3 us -> none  [local(): portion = lax.all_gather(direction, 'row', axis=0, tiled=True)]
    all_to_all x0 -> x1, starting transfers between devices: none -> 5.57 us  [local(): lax.all_to_all(jnp.stack([direction] * lax.axis_size('row')), 'row', 0, 0)]
    reduce_scatter x1, waiting for transfers between devices: 74.2 us -> 78.4 us  [local(): lax.psum_scatter(lax.dot_general(columns, hidden, (((0,), (0,)), ((), ())...]
    another operation x0 -> x1, local copies, waits for them, and re-layouts: none -> 3.61 us  [local(): jnp.stack([direction] * lax.axis_size('row'))]
  transfers between devices with their start and end apart: 3 -> 3, of which waited for: 3 -> 2; matrix products, arithmetic and copies ran while one was open for 4% -> 1% of each run, Pallas kernels for 0% -> 0%
where the time goes in v2:
time: 348 us
  waiting for transfers between devices  176 us (51%)
  blocking collectives  90.6 us (26%)
  matrix products  43.1 us (12%)
  between operations  15.5 us (4%)
  other arithmetic  11.4 us (3%)
  starting transfers between devices  5.83 us (2%)
  local copies, waits for them, and re-layouts  5.16 us (1%)
    psum x1, waiting for transfers between devices, spread(): return lax.psum(block, axis)  98.1 us
    psum x1, blocking collectives, local(): projected = lax.psum(partial_value, 'col').astype(jnp.bfloat16)  90.6 us
    reduce_scatter x1, waiting for transfers between devices, local(): lax.psum_scatter(lax.dot_general(columns, hidden, (((0,), (0,)), ((), ())...  78.4 us
    dot_general x1, matrix products, local(): jnp.dot(columns, portion, preferred_element_type=jnp.float32)  24.2 us
    dot_general x1, matrix products, local(): lax.dot_general(columns, hidden, (((0,), (0,)), ((), ())), preferred_elem...  13 us
    convert_element_type x1, other arithmetic, local(): (first_hat / (jnp.sqrt(second_hat) + epsilon)).astype(jnp.bfloat16)  9.05 us
  transfers between devices with their start and end apart: 3, of which 2 were waited for; matrix products, arithmetic and copies ran while one was open for 1% of the time, Pallas kernels for 0%

profile of v2, /device:TPU:0, one launch (start us, length us, event | category | flops | bytes accessed | tf_op | source)
XLA Modules:
  0.0 348.1 jit_solution(5711235727999492757)
XLA Ops:
  8.0 0.0 copy-start
  8.0 0.0 reduce-scatter.2.cloned.1.call-start
  8.1 1.5 copy-done
  9.6 5.9 %fusion.9 = f32[1024,1024]{1,0:T(8,128)} fusion(bf16[1024,1024]{1,0:T(8,128)(2,1)S(1)} %copy-done, bf16[1024,1024]{1,0:T(8,128)(2,1)} %param.8), kind=kOutput, calls=%fused_computation.14 | convolution fusion | flops 2147483648 | bytes 8388608 | tf_op jit(solution)/shard_map/dot_general | solution.py:19
  15.5 90.6 %all-reduce.5 = bf16[1024,1024]{1,0:T(8,128)(2,1)S(1)} all-reduce(f32[1024,1024]{1,0:T(8,128)} %fusion.9), channel_id=1, replica_groups=mesh['row'=4,'col'=8] {'col'}, use_global_device_ids=true, to_apply=%region_2.3 | all-reduce | flops 1048576 | bytes 6291456 | tf_op jit(solution)/shard_map/psum | solution.py:20
  106.1 13.0 %convolution_convert_fusion = bf16[1024,3584]{1,0:T(8,128)(2,1)} fusion(bf16[1024,3584]{1,0:T(8,128)(2,1)} %param.7, bf16[1024,1024]{1,0:T(8,128)(2,1)S(1)} %all-reduce.5), kind=kOutput, calls=%fused_computation.1 | convolution fusion | flops 7519862784 | bytes 16777216 | tf_op jit(solution)/shard_map/dot_general | solution.py:23
  119.1 0.0 reduce-scatter.2.cloned.1.call-update
  119.1 78.4 %reduce-scatter.2.cloned.1.call-done = bf16[256,3584]{1,0:T(8,128)(2,1)} async-done(((bf16[1024,3584]{1,0:T(8,128)(2,1)}), bf16[256,3584]{1,0:T(8,128)(2,1)}) %reduce-scatter.2.cloned.1.call-update) | async-done | bytes 1835024 | tf_op jit(solution)/shard_map/reduce_scatter | solution.py:22
  197.5 9.0 %divide_convert_fusion = (bf16[256,3584]{1,0:T(8,128)(2,1)S(1)}, f32[256,3584]{1,0:T(8,128)}, f32[256,3584]{1,0:T(8,128)}) fusion(bf16[256,3584]{1,0:T(8,128)(2,1)} %reduce-scatter.2.cloned.1.call-done, f32[256,3584]{1,0:T(8,128)} %param.11, f32[256,3584]{1,0:T(8,128)} %param.10), kind=kLoop, calls=%fused_computation.9 | loop fusion | flops 11010048 | bytes 18350080 | tf_op jit(solution)/shard_map/convert_element_type | solution.py:34
  206.6 3.6 %stack.2 = bf16[4,256,3584]{2,1,0:T(8,128)(2,1)} broadcast(bf16[256,3584]{1,0:T(8,128)(2,1)S(1)} %get-tuple-element.5), dimensions={1,2} | broadcast | bytes 9175040 | tf_op jit(solution)/shard_map/stack | solution.py:43
  210.2 0.0 copy-start.2
  210.2 5.6 %all-to-all-start = ((bf16[4,256,3584]{2,1,0:T(8,128)(2,1)}), bf16[4,256,3584]{2,1,0:T(8,128)(2,1)}, u32[]{:S(2)}, u32[]{:S(2)}) async-start(bf16[4,256,3584]{2,1,0:T(8,128)(2,1)} %stack.2), calls=%async_computation.1 | async-start | bytes 14680064 | tf_op jit(solution)/shard_map/all_to_all | solution.py:43
  215.8 0.2 all-reduce.4.cloned.1.call-start
  216.0 0.0 copy-done.2
  216.0 2.3 broadcast_select_fusion.1
  218.3 0.0 all-reduce.4.cloned.1.call-update
  218.4 98.1 %all-reduce.4.cloned.1.call-done = (bf16[1024,1024]{1,0:T(8,128)(2,1)}, bf16[1024,1024]{1,0:T(8,128)(2,1)}) async-done(((bf16[1024,1024]{1,0:T(8,128)(2,1)}, bf16[1024,1024]{1,0:T(8,128)(2,1)}), (bf16[1024,1024]{1,0:T(8,128)(2,1)}, bf16[1024,1024]{1,0:T(8,128)(2,1)})) %all-reduce.4.cloned.1.call-update) | async-done | bytes 4194320 | tf_op jit(solution)/shard_map/psum | solution.py:15
  316.4 0.0 all-to-all-done
  316.4 0.0 copy-start.1
  316.4 24.2 %subtract_convert_fusion = bf16[2048,3584]{1,0:T(8,128)(2,1)} fusion(bf16[2048,3584]{1,0:T(8,128)(2,1)} %param.9, bf16[1024,3584]{1,0:T(8,128)(2,1)} %bitcast, bf16[1024,1024]{1,0:T(8,128)(2,1)} %get-tuple-element.3, bf16[1024,1024]{1,0:T(8,128)(2,1)} %get-tuple-element.4), kind=kOutput, calls=%fused_computation | convolution fusion | flops 15062794240 | bytes 40894464 | tf_op jit(solution)/shard_map/dot_general | solution.py:46
  340.7 0.0 copy-done.1
Async XLA Ops:
  8.0 1.6 copy-start
  8.0 189.5 %reduce-scatter.2.cloned.1.call-start = ((), (), s32[]{:S(2)}) async-start(), calls=%async_computation.2 | async-start | bytes 9175040 | tf_op jit(solution)/shard_map/reduce_scatter | solution.py:22
  210.2 5.8 %copy-start.2 = (bf16[1024,1024]{1,0:T(8,128)(2,1)S(1)}, bf16[1024,1024]{1,0:T(8,128)(2,1)}, u32[]{:S(2)}) copy-start(bf16[1024,1024]{1,0:T(8,128)(2,1)} %param.8) | copy-start | bytes 6291460
  210.2 106.2 %all-to-all-start = ((bf16[4,256,3584]{2,1,0:T(8,128)(2,1)}), bf16[4,256,3584]{2,1,0:T(8,128)(2,1)}, u32[]{:S(2)}, u32[]{:S(2)}) async-start(bf16[4,256,3584]{2,1,0:T(8,128)(2,1)} %stack.2), calls=%async_computation.1 | async-start | bytes 14680064 | tf_op jit(solution)/shard_map/all_to_all | solution.py:43
  215.8 100.7 %all-reduce.4.cloned.1.call-start = ((), (), s32[]{:S(2)}) async-start(), calls=%async_computation.3 | async-start | bytes 8388608 | tf_op jit(solution)/shard_map/psum | solution.py:15
  316.4 24.2 %copy-start.1 = (bf16[1024,1024]{1,0:T(8,128)(2,1)S(1)}, bf16[1024,1024]{1,0:T(8,128)(2,1)}, u32[]{:S(2)}) copy-start(bf16[1024,1024]{1,0:T(8,128)(2,1)} %param.6) | copy-start | bytes 6291460
Sparse Core Ops, SparseCore 0:
  119.3 78.2 reduce-scatter.1
Sparse Core Ops, SparseCore 1:
  218.7 97.7 all-reduce.3
